TPU v7x, 256 devices: a whole 4x4x8 slice. The times are simulated.
256 devices in a mesh: ctx: 32 (over z_hi, y, x), ch: 8 (over z_lo, core).
Axes of the slice: x: 4, y: 4, z: 8 (z_hi: 2, z_lo: 4; z = z_hi * 4 + z_lo), core: 2. Of those that a mesh axis runs over, the one named last changes fastest.
Arguments:
- grad_out: bfloat16 [24576, 4096], P('ctx', 'ch'), may hold values from -6 to 6
- block_input: bfloat16 [24576, 4096], P('ctx', 'ch'), may hold values from -40 to 40
- norm_gain: bfloat16 [4096], P('ch'), may hold values from 0.5 to 1.5
- queries: bfloat16 [24576, 4096], P('ctx', 'ch'), may hold values from -6 to 6
- keys: bfloat16 [24576, 4096], P('ctx', 'ch'), may hold values from -6 to 6
- values: bfloat16 [24576, 4096], P('ctx', 'ch'), may hold values from -6 to 6
- filters: bfloat16 [256, 128], P('ch'), may hold values from -0.5 to 0.5
- doc_starts: int32 [32, 4], P('ctx'), may hold values from 0 to 767, as said below
- in_weight: bfloat16 [4096, 3, 4096], P('ctx', None, 'ch'), may hold values from -0.09375 to 0.09375
- out_weight: bfloat16 [4096, 4096], P('ch', 'ctx'), may hold values from -0.09375 to 0.09375
Outputs:
- grad_input: bfloat16 [24576, 4096], P('ctx', 'ch')
Inputs may be any that keep to these rules, and one draw needn't show every extreme that they name: `doc_starts`: each row holds 4 distinct document starts of one slab as offsets within the slab, in ascending order; the first slab's first start is 0.
All inputs are finite; a program needn't handle non-finite values.
Results may differ from a plain program's by a relative error of at most 0.013.
Values may be sent and summed in bfloat16 or wider, within the bound.
A program may use at most 128 MiB of HBM per device.

v0:
```python
import jax
import jax.numpy as jnp
from jax import lax
from jax.sharding import PartitionSpec as P

D = 4096
FILTER_LEN = 128
GROUP_WIDTH = 16
DOCS = 4
epsilon = 1e-05


def shifted(block, axis, distance):
    devices = range(lax.axis_size(axis))
    route = [(i - distance, i) for i in devices if i - distance in devices]
    return lax.ppermute(block, axis, route)


def on_device(
    grad_out,
    block_input,
    norm_gain,
    queries,
    keys,
    values,
    filters,
    doc_starts,
    in_weight,
    out_weight,
):
    tok_rows = grad_out.shape[0]
    chan_width = grad_out.shape[1]
    group_count = filters.shape[0]
    tile_count = tok_rows // FILTER_LEN
    source_in = block_input.astype(jnp.float32)
    square_sum = lax.psum(jnp.sum(source_in * source_in, axis=1), "ch")
    starts = doc_starts[0]
    positions = jnp.arange(tok_rows, dtype=jnp.int32)
    own_last = jnp.max(
        jnp.where(starts[None, :] <= positions[:, None], starts[None, :], -tok_rows), axis=1
    )
    products = (keys.astype(jnp.float32) * values.astype(jnp.float32)).astype(jnp.bfloat16)
    tail_rows, prior_start = shifted(
        (products[tok_rows - FILTER_LEN :], starts[DOCS - 1 :]), "ctx", 1
    )
    last_start = jnp.maximum(own_last, prior_start[0] - tok_rows)
    tap_index = (
        jnp.arange(FILTER_LEN, dtype=jnp.int32)[:, None]
        + FILTER_LEN
        - jnp.arange(2 * FILTER_LEN, dtype=jnp.int32)[None, :]
    )
    selector = (jnp.arange(FILTER_LEN, dtype=jnp.int32)[:, None, None] == tap_index[None]).astype(
        jnp.bfloat16
    )
    selector = selector.reshape(FILTER_LEN, 2 * FILTER_LEN * FILTER_LEN)
    table = jnp.dot(filters, selector, preferred_element_type=jnp.float32).astype(jnp.bfloat16)
    table = table.reshape(group_count, FILTER_LEN, 2 * FILTER_LEN)
    flipped = table[:, ::-1, ::-1]
    padded_prod = jnp.concatenate([tail_rows, products], axis=0)

    def forward_tile(tile_idx):
        source = lax.dynamic_slice_in_dim(padded_prod, tile_idx * FILTER_LEN, 2 * FILTER_LEN, 0)
        source = source.reshape(2 * FILTER_LEN, group_count, GROUP_WIDTH)
        row_last = lax.dynamic_slice_in_dim(last_start, tile_idx * FILTER_LEN, FILTER_LEN, 0)
        col_pos = (tile_idx - 1) * FILTER_LEN + jnp.arange(2 * FILTER_LEN, dtype=jnp.int32)
        allowed = col_pos[None, :] >= row_last[:, None]
        masked = jnp.where(allowed[None], table, jnp.zeros_like(table))
        return jnp.einsum(
            "gtp,pgc->tgc", masked, source, preferred_element_type=jnp.float32
        ).reshape(FILTER_LEN, chan_width)

    mixed = lax.map(forward_tile, jnp.arange(tile_count, dtype=jnp.int32)).reshape(
        tok_rows, chan_width
    )
    gathered = lax.all_gather(grad_out, "ch", axis=1, tiled=True)
    mix_grad = lax.dot_general(
        gathered,
        lax.all_gather(out_weight, "ctx", axis=1, tiled=True),
        (((1,), (1,)), ((), ())),
        preferred_element_type=jnp.float32,
    )
    q_grad = (mix_grad * mixed).astype(jnp.bfloat16)
    w_grad = (mix_grad * queries.astype(jnp.float32)).astype(jnp.bfloat16)
    head_rows, head_last = shifted((w_grad[:FILTER_LEN], last_start[:FILTER_LEN]), "ctx", -1)
    padded_grad = jnp.concatenate([w_grad, head_rows], axis=0)
    padded_last = jnp.concatenate([last_start, head_last + tok_rows], axis=0)

    def backward_tile(tile_idx):
        source = lax.dynamic_slice_in_dim(padded_grad, tile_idx * FILTER_LEN, 2 * FILTER_LEN, 0)
        source = source.reshape(2 * FILTER_LEN, group_count, GROUP_WIDTH)
        col_last = lax.dynamic_slice_in_dim(padded_last, tile_idx * FILTER_LEN, 2 * FILTER_LEN, 0)
        row_pos = tile_idx * FILTER_LEN + jnp.arange(FILTER_LEN, dtype=jnp.int32)
        allowed = row_pos[:, None] >= col_last[None, :]
        masked = jnp.where(allowed[None], flipped, jnp.zeros_like(flipped))
        return jnp.einsum(
            "gst,tgc->sgc", masked, source, preferred_element_type=jnp.float32
        ).reshape(FILTER_LEN, chan_width)

    conv_grad = lax.map(backward_tile, jnp.arange(tile_count, dtype=jnp.int32)).reshape(
        tok_rows, chan_width
    )
    k_grad = (conv_grad * values.astype(jnp.float32)).astype(jnp.bfloat16)
    v_grad = (conv_grad * keys.astype(jnp.float32)).astype(jnp.bfloat16)
    stacked = jnp.stack([q_grad, k_grad, v_grad], axis=1).reshape(tok_rows, 3 * chan_width)
    weight_rows = lax.all_gather(in_weight, "ctx", axis=0, tiled=True)
    flat_rows = weight_rows.reshape(weight_rows.shape[0], 3 * chan_width)
    hidden_terms = lax.dot_general(
        stacked, flat_rows, (((1,), (1,)), ((), ())), preferred_element_type=jnp.float32
    )
    norm_grad = lax.psum_scatter(
        hidden_terms.astype(jnp.bfloat16), "ch", scatter_dimension=1, tiled=True
    ).astype(jnp.float32)
    scaled = norm_gain.astype(jnp.float32)[None, :] * norm_grad
    cross_sum = lax.psum(jnp.sum(scaled * source_in, axis=1), "ch")
    inverse = lax.rsqrt(square_sum / D + epsilon)[:, None]
    result = (
        grad_out.astype(jnp.float32)
        + inverse * scaled
        - source_in * (inverse * inverse * inverse) * cross_sum[:, None] / D
    )
    return result.astype(jnp.bfloat16)


def solution(mesh):
    placed = (
        P("ctx", "ch"),
        P("ctx", "ch"),
        P("ch"),
        P("ctx", "ch"),
        P("ctx", "ch"),
        P("ctx", "ch"),
        P("ch", None),
        P("ctx", None),
        P("ctx", None, "ch"),
        P("ch", "ctx"),
    )
    return jax.shard_map(
        on_device, mesh=mesh, in_specs=placed, out_specs=P("ctx", "ch"), check_vma=False
    )
```

profile of v0, /device:TPU:1, one launch (start us, length us, event | category | flops | bytes accessed | tf_op | source)
XLA Modules:
  0.0 529.9 jit_solution(16419598484490058867)
XLA Ops:
  6.5 0.7 all-gather.6.cloned.1.call-update
  7.3 0.7 all-gather.4.cloned.1.call-update
  8.1 0.7 all-gather.8.cloned.1.call-update
  8.8 1.3 fusion.17
  10.2 3.9 collective-permute-start
  14.1 0.6 slice.16
  14.7 3.6 collective-permute-start.1
  18.7 3.5 convolution_convert_fusion
  22.2 0.5 copy.28
  22.7 22.6 %rev.3 = bf16[32,128,256]{2,1,0:T(8,128)(2,1)} reverse(bf16[32,128,256]{2,1,0:T(8,128)(2,1)S(1)} %bitcast.57), dimensions={1,2} | reverse | bytes 4194304 | tf_op jit(solution)/shard_map/rev | solution.py:58
  46.0 1.3 collective-permute-start.3
  47.3 1.0 pad_maximum_fusion
  48.3 1.4 broadcast.91.clone2
  49.7 28.5 %while.22 = (s32[]{:T(128)}, f32[6,128,512]{2,1,0:T(8,128)}, s32[6]{0:T(128)S(1)}, bf16[896,512]{1,0:T(8,128)(2,1)}, s32[768]{0:T(1024)S(1)}, /*index=5*/bf16[32...) while((s32[]{:T(128)}, f32[6,128,512]{2,1,0:T(8,128)}, ...), condition=%wide.region_4.5_spmd, body=%wide.region_3.4_spmd.sunk | while | flops 34636040 | bytes 4788460 | solution.py:72
  49.7 0.6 dynamic_slice.37
  51.8 1.0 constant_dynamic-slice_fusion.4
  52.9 0.6 fusion.41
  53.7 0.7 constant_dynamic-update-slice_fusion.4
  54.4 0.6 dynamic_slice.37
  56.5 1.0 constant_dynamic-slice_fusion.4
  57.7 0.6 fusion.41
  58.5 0.7 constant_dynamic-update-slice_fusion.4
  59.2 0.6 dynamic_slice.37
  61.3 1.0 constant_dynamic-slice_fusion.4
  62.4 0.6 fusion.41
  63.2 0.7 constant_dynamic-update-slice_fusion.4
  63.9 0.6 dynamic_slice.37
  66.0 1.0 constant_dynamic-slice_fusion.4
  67.2 0.7 fusion.41
  68.0 0.7 constant_dynamic-update-slice_fusion.4
  68.7 0.6 dynamic_slice.37
  70.8 1.0 constant_dynamic-slice_fusion.4
  71.9 0.6 fusion.41
  72.7 0.7 constant_dynamic-update-slice_fusion.4
  73.4 0.6 dynamic_slice.37
  75.5 1.0 constant_dynamic-slice_fusion.4
  76.6 0.6 fusion.41
  77.4 0.7 constant_dynamic-update-slice_fusion.4
  78.2 68.1 %all-gather.6.cloned.1.call-done = bf16[512,4096]{1,0:T(8,128)(2,1)} async-done(((bf16[512,128]{1,0:T(8,128)(2,1)}), bf16[512,4096]{1,0:T(8,128)(2,1)}) %all-gather.6.cloned.1.call-update) | async-done | bytes 4194320 | tf_op jit(solution)/shard_map/all_gather | solution.py:78
  146.2 71.0 %all-gather.4.cloned.1.call-done = bf16[768,4096]{1,0:T(8,128)(2,1)} async-done(((bf16[768,512]{1,0:T(8,128)(2,1)}), bf16[768,4096]{1,0:T(8,128)(2,1)}) %all-gather.4.cloned.1.call-update) | async-done | bytes 6291472 | tf_op jit(solution)/shard_map/all_gather | solution.py:75
  217.3 9.0 %fusion.25 = (bf16[768,512]{1,0:T(8,128)(2,1)}, bf16[768,512]{1,0:T(8,128)(2,1)S(1)}) fusion(f32[6,128,512]{2,1,0:T(8,128)} %get-tuple-element.114, bf16[768,512]{1,0:T(8,128)(2,1)} %param.17, bf16[768,4096]{1,0:T(8,128)(2,1)} %all-gather.4.cloned.1.call-done, bf16[512,4096]{1,0:T(8,128)(2,1)} %all-gather.6.cloned.1.call-done), kind=kOutput, calls=%fused_computation.43 | convolution fusion | flops 3223191552 | bytes 14417920 | tf_op jit(solution)/shard_map/dot_general | solution.py:76
  226.3 1.5 collective-permute-start.2
  227.8 4.2 collective-permute-done.2
  232.2 23.9 %while.23 = (s32[]{:T(128)}, f32[6,128,512]{2,1,0:T(8,128)S(1)}, s32[6]{0:T(128)S(1)}, bf16[896,512]{1,0:T(8,128)(2,1)S(1)}, s32[896]{0:T(1024)S(1)}, /*index=5*...) while((s32[]{:T(128)}, f32[6,128,512]{2,1,0:T(8,128)S(1)}, s32[6]{0:T(128)S(1)}, ...), condition=%wide.region_6.7_spmd, body=%wide.region_5.6_spmd.sunk | while | flops 34635908 | bytes 4788399 | solution.py:99
  232.2 0.6 dynamic_slice.40
  233.8 2.4 fusion.44
  236.3 0.6 dynamic_slice.40
  237.8 2.2 fusion.44
  240.3 0.6 dynamic_slice.40
  241.8 2.2 fusion.44
  244.2 0.6 dynamic_slice.40
  245.7 2.2 fusion.44
  248.2 0.6 dynamic_slice.40
  249.7 2.2 fusion.44
  252.2 0.6 dynamic_slice.40
  253.7 2.2 fusion.44
  256.1 1.8 fusion.18
  257.9 163.2 %all-gather.8.cloned.1.call-done = bf16[4096,3,512]{2,0,1:T(8,128)(2,1)} async-done(((bf16[128,3,512]{2,0,1:T(8,128)(2,1)}), bf16[4096,3,512]{2,0,1:T(8,128)(2,1)}) %all-gather.8.cloned.1.call-update) | async-done | bytes 12582928 | tf_op jit(solution)/shard_map/all_gather | solution.py:105
  421.1 14.8 %bitcast_convert_fusion = bf16[768,4096]{1,0:T(8,128)(2,1)} fusion(bf16[4096,3,512]{2,0,1:T(8,128)(2,1)} %all-gather.8.cloned.1.call-done, bf16[768,1,512]{2,0,1:T(8,128)(2,1)S(1)} %bitcast.65, bf16[768,1,512]{2,0,1:T(8,128)(2,1)S(1)} %bitcast.64, bf16[768,1,512]{2,0,1:T(8,128)(2,1)} %bitcast.69), kind=kOutput, calls=%fused_computation.20 | convolution fusion | flops 9669181440 | bytes 21233664 | tf_op jit(solution)/shard_map/dot_general | solution.py:107
  435.9 0.7 copy-done.5
  436.5 67.7 %reduce-scatter.2.cloned.1.call-done = bf16[768,512]{1,0:T(8,128)(2,1)} async-done(((bf16[768,4096]{1,0:T(8,128)(2,1)}), bf16[768,512]{1,0:T(8,128)(2,1)}) %reduce-scatter.2.cloned.1.call-update) | async-done | bytes 786448 | tf_op jit(solution)/shard_map/reduce_scatter | solution.py:110
  504.3 1.6 fusion.19
  505.9 16.0 %all-reduce = (f32[768]{0:T(1024)S(1)}, f32[768]{0:T(1024)S(1)}) all-reduce(f32[768]{0:T(1024)S(1)} %get-tuple-element.141, f32[768]{0:T(1024)S(1)} %get-tuple-element.140), channel_id=1, replica_groups=mesh['ctx'=32,'ch'=8] {'ch'}, use_global_device_ids=true, to_apply=%region_9.10 | all-reduce | flops 1536 | bytes 12288 | tf_op jit(solution)/shard_map/psum | solution.py:114
  521.9 1.5 fusion.23
  (111 shorter events, 6.6 us)
Async XLA Ops:
  6.5 12.1 %copy-start = (bf16[32,128]{1,0:T(8,128)(2,1)S(1)}, bf16[32,128]{1,0:T(8,128)(2,1)}, u32[]{:S(2)}) copy-start(bf16[32,128]{1,0:T(8,128)(2,1)} %param.20) | copy-start | bytes 24580
  6.5 2.3 copy-start.1
  6.5 139.7 %all-gather.6.cloned.1.call-start = ((), (), s32[]{:S(2)}) async-start(), calls=%async_computation.2 | async-start | bytes 4325376 | tf_op jit(solution)/shard_map/all_gather | solution.py:78
  7.3 210.0 %all-gather.4.cloned.1.call-start = ((), (), s32[]{:S(2)}) async-start(), calls=%async_computation.1 | async-start | bytes 7077888 | tf_op jit(solution)/shard_map/all_gather | solution.py:75
  8.0 6.1 %copy-start.6 = (s32[1,4]{1,0:T(1,128)S(1)}, s32[1,4]{1,0:T(1,128)}, u32[]{:S(2)}) copy-start(s32[1,4]{1,0:T(1,128)} %param.21) | copy-start | bytes 52
  8.0 413.0 %all-gather.8.cloned.1.call-start = ((), (), s32[]{:S(2)}) async-start(), calls=%async_computation.3 | async-start | bytes 12976128 | tf_op jit(solution)/shard_map/all_gather | solution.py:105
  8.8 495.5 %reduce-scatter.2.cloned.1.call-start = ((), (), s32[]{:S(2)}) async-start(), calls=%async_computation.4 | async-start | bytes 7077888 | tf_op jit(solution)/shard_map/reduce_scatter | solution.py:110
  10.2 37.1 %collective-permute-start = (bf16[128,512]{1,0:T(8,128)(2,1)S(1)}, bf16[128,512]{1,0:T(8,128)(2,1)S(1)}, u32[]{:S(2)}, u32[]{:S(2)}) collective-permute-start(bf16[128,512]{1,0:T(8,128)(2,1)S(1)} %slice.20), channel_id=1, source_target_pairs={{0,8},{8,16},{16,24},{24,32},{32,40},{40,48},{48,56},{56,64},{64,7... | collective-permute-start | bytes 393224 | tf_op jit(solution)/shard_map/ppermute | solution.py:16
  14.7 30.6 %collective-permute-start.1 = (s32[1]{0:T(128)}, s32[1]{0:T(128)}, u32[]{:S(2)}, u32[]{:S(2)}) collective-permute-start(s32[1]{0:T(128)} %bitcast.10), channel_id=1, source_target_pairs={{0,8},{8,16},{16,24},{24,32},{32,40},{40,48},{48,56},{56,64},{64,7... | collective-permute-start | bytes 20 | tf_op jit(solution)/shard_map/ppermute | solution.py:16
  46.0 181.8 %collective-permute-start.3 = (s32[128]{0:T(128)S(1)}, s32[128]{0:T(128)S(1)}, u32[]{:S(2)}, u32[]{:S(2)}) collective-permute-start(s32[128]{0:T(128)S(1)} %slice.19), channel_id=1, source_target_pairs={{8,0},{16,8},{24,16},{32,24},{40,32},{48,40},{56,48},{64,56},{72,6... | collective-permute-start | bytes 1544 | tf_op jit(solution)/shard_map/ppermute | solution.py:16
  226.3 5.7 %collective-permute-start.2 = (bf16[128,512]{1,0:T(8,128)(2,1)S(1)}, bf16[128,512]{1,0:T(8,128)(2,1)S(1)}, u32[]{:S(2)}, u32[]{:S(2)}) collective-permute-start(bf16[128,512]{1,0:T(8,128)(2,1)S(1)} %slice.21), channel_id=1, source_target_pairs={{8,0},{16,8},{24,16},{32,24},{40,32},{48,40},{56,48},{64,56},{72,6... | collective-permute-start | bytes 393224 | tf_op jit(solution)/shard_map/ppermute | solution.py:16
  435.8 0.7 copy-start.5
  435.8 68.4 %copy-start.2 = (bf16[768,512]{1,0:T(8,128)(2,1)S(1)}, bf16[768,512]{1,0:T(8,128)(2,1)}, u32[]{:S(2)}) copy-start(bf16[768,512]{1,0:T(8,128)(2,1)} %param.15) | copy-start | bytes 2359300
  436.5 85.4 %copy-start.3 = (bf16[768,512]{1,0:T(8,128)(2,1)S(1)}, bf16[768,512]{1,0:T(8,128)(2,1)}, u32[]{:S(2)}) copy-start(bf16[768,512]{1,0:T(8,128)(2,1)} %param.14) | copy-start | bytes 2359300
  504.3 17.7 %copy-start.4 = (bf16[768,512]{1,0:T(8,128)(2,1)S(1)}, bf16[768,512]{1,0:T(8,128)(2,1)}, u32[]{:S(2)}) copy-start(bf16[768,512]{1,0:T(8,128)(2,1)} %reduce-scatter.2.cloned.1.call-done) | copy-start | bytes 2359300
Sparse Core Ops, SparseCore 0:
  10.5 135.6 all-gather.5
  148.0 69.2 all-gather.3
  220.8 200.1 all-gather.7
  436.0 68.2 reduce-scatter.1
where the time goes:
time: 531 us; the launch traced here: 530 us
  waiting for transfers between devices  376 us (71%)
  local copies, waits for them, and re-layouts  48.3 us (9%)
  matrix products  44.6 us (8%)
  blocking collectives  16 us (3%)
  between operations  13.9 us (3%)
  loops' own time  11.8 us (2%)
  starting transfers between devices  10.4 us (2%)
  other arithmetic  8.54 us (2%)
    all_gather x1, waiting for transfers between devices, on_device(): weight_rows = lax.all_gather(in_weight, 'ctx', axis=0, tiled=True)  163 us
    all_gather x1, waiting for transfers between devices, on_device(): gathered = lax.all_gather(grad_out, 'ch', axis=1, tiled=True)  71 us
    all_gather x1, waiting for transfers between devices, on_device(): lax.all_gather(out_weight, 'ctx', axis=1, tiled=True)  68.1 us
    reduce_scatter x1, waiting for transfers between devices, on_device(): lax.psum_scatter(hidden_terms.astype(jnp.bfloat16), 'ch', scatter_dimensi...  67.7 us
    rev x1, local copies, waits for them, and re-layouts, on_device(): flipped = table[:, ::-1, ::-1]  22.6 us
    psum x1, blocking collectives, on_device(): cross_sum = lax.psum(jnp.sum(scaled * source_in, axis=1), 'ch')  16 us
    dot_general x1, matrix products, on_device(): lax.dot_general(stacked, flat_rows, (((1,), (1,)), ((), ())), preferred_e...  14.8 us
    dot_general x6, matrix products, backward_tile(): jnp.einsum('gst,tgc->sgc', masked, source, preferred_element_type=jnp.flo...  13.6 us
  transfers between devices with their start and end apart: 8, of which 5 were waited for; matrix products, arithmetic and copies ran while one was open for 16% of the time, Pallas kernels for 0%

commit v1 on v0

--- a/solution.py
+++ b/solution.py
@@ -75,7 +75,9 @@
     gathered = lax.all_gather(grad_out, "ch", axis=1, tiled=True)
     mix_grad = lax.dot_general(
         gathered,
-        lax.all_gather(out_weight, "ctx", axis=1, tiled=True),
+        jnp.concatenate(
+            lax.all_to_all(jnp.stack([out_weight] * lax.axis_size("ctx")), "ctx", 0, 0), axis=1
+        ),
         (((1,), (1,)), ((), ())),
         preferred_element_type=jnp.float32,
     )

time: 531 us -> 491 us (0.925)
  waiting for transfers between devices: 376 us -> 318 us
  starting transfers between devices: 10.4 us -> 24.3 us
    all_to_all x0 -> x1, waiting for transfers between devices: none -> 71.6 us  [on_device(): lax.all_to_all(jnp.stack([out_weight] * lax.axis_size('ctx')), 'ctx', 0, 0)]
    all_gather x1 -> x0, waiting for transfers between devices: 68.1 us -> none  [on_device(): lax.all_gather(out_weight, 'ctx', axis=1, tiled=True)]
    all_gather x1, waiting for transfers between devices: 71 us -> 8.81 us  [on_device(): gathered = lax.all_gather(grad_out, 'ch', axis=1, tiled=True)]
    all_to_all x0 -> x1, starting transfers between devices: none -> 14.7 us  [on_device(): lax.all_to_all(jnp.stack([out_weight] * lax.axis_size('ctx')), 'ctx', 0, 0)]
  transfers between devices with their start and end apart: 8 -> 8, of which waited for: 5 -> 5; matrix products, arithmetic and copies ran while one was open for 16% -> 18% of each run, Pallas kernels for 0% -> 0%
where the time goes in v1:
time: 491 us; the launch traced here: 490 us
  waiting for transfers between devices  318 us (65%)
  local copies, waits for them, and re-layouts  52.5 us (11%)
  matrix products  44.6 us (9%)
  starting transfers between devices  24.3 us (5%)
  blocking collectives  16 us (3%)
  between operations  14 us (3%)
  loops' own time  12.7 us (3%)
  other arithmetic  7.38 us (2%)
    all_gather x1, waiting for transfers between devices, on_device(): weight_rows = lax.all_gather(in_weight, 'ctx', axis=0, tiled=True)  164 us
    all_to_all x1, waiting for transfers between devices, on_device(): lax.all_to_all(jnp.stack([out_weight] * lax.axis_size('ctx')), 'ctx', 0, 0)  71.6 us
    reduce_scatter x1, waiting for transfers between devices, on_device(): lax.psum_scatter(hidden_terms.astype(jnp.bfloat16), 'ch', scatter_dimensi...  67.7 us
    rev x1, local copies, waits for them, and re-layouts, on_device(): flipped = table[:, ::-1, ::-1]  22.6 us
    psum x1, blocking collectives, on_device(): cross_sum = lax.psum(jnp.sum(scaled * source_in, axis=1), 'ch')  16 us
    dot_general x1, matrix products, on_device(): lax.dot_general(stacked, flat_rows, (((1,), (1,)), ((), ())), preferred_e...  14.8 us
    all_to_all x1, starting transfers between devices, on_device(): lax.all_to_all(jnp.stack([out_weight] * lax.axis_size('ctx')), 'ctx', 0, 0)  14.7 us
    dot_general x6, matrix products, backward_tile(): jnp.einsum('gst,tgc->sgc', masked, source, preferred_element_type=jnp.flo...  13.6 us
  transfers between devices with their start and end apart: 8, of which 5 were waited for; matrix products, arithmetic and copies ran while one was open for 18% of the time, Pallas kernels for 0%

profile of v1, /device:TPU:1, one launch (start us, length us, event | category | flops | bytes accessed | tf_op | source)
XLA Modules:
  0.0 489.7 jit_solution(8426792551903206693)
XLA Ops:
  6.5 0.7 all-gather.3.cloned.1.call-update
  7.3 0.7 all-gather.5.cloned.1.call-update
  8.0 1.0 copy.20
  9.0 2.5 stack.10
  11.5 14.7 %all-to-all-start = ((bf16[32,512,128]{1,2,0:T(8,128)(2,1)}), bf16[32,512,128]{1,2,0:T(8,128)(2,1)}, u32[]{:S(2)}, u32[]{:S(2)}) async-start(bf16[32,512,128]{1,2,0:T(8,128)(2,1)} %stack.10), calls=%async_computation | async-start | bytes 8388608 | tf_op jit(solution)/shard_map/all_to_all | solution.py:79
  26.6 3.1 collective-permute-start
  29.7 0.7 slice.16
  30.3 3.6 collective-permute-start.1
  34.3 3.5 convolution_convert_fusion
  38.3 22.6 %rev.3 = bf16[32,128,256]{2,1,0:T(8,128)(2,1)} reverse(bf16[32,128,256]{2,1,0:T(8,128)(2,1)S(1)} %bitcast.60), dimensions={1,2} | reverse | bytes 4194304 | tf_op jit(solution)/shard_map/rev | solution.py:58
  61.7 1.3 collective-permute-start.3
  63.0 1.0 pad_maximum_fusion
  64.0 1.4 broadcast.93.clone2
  65.4 29.1 %while.22 = (s32[]{:T(128)}, f32[6,128,512]{2,1,0:T(8,128)}, s32[6]{0:T(128)S(1)}, bf16[896,512]{1,0:T(8,128)(2,1)}, s32[768]{0:T(1024)S(1)}, /*index=5*/bf16[32...) while((s32[]{:T(128)}, f32[6,128,512]{2,1,0:T(8,128)}, ...), condition=%wide.region_4.5_spmd, body=%wide.region_3.4_spmd.sunk | while | flops 34636040 | bytes 4788460 | solution.py:72
  65.4 0.7 dynamic_slice.37
  67.6 1.0 constant_dynamic-slice_fusion.4
  68.7 0.6 fusion.41
  69.5 0.7 constant_dynamic-update-slice_fusion.4
  70.3 0.7 dynamic_slice.37
  72.5 1.0 constant_dynamic-slice_fusion.4
  73.6 0.6 fusion.41
  74.4 0.7 constant_dynamic-update-slice_fusion.4
  75.1 0.7 dynamic_slice.37
  77.3 1.0 constant_dynamic-slice_fusion.4
  78.5 0.6 fusion.41
  79.3 0.7 constant_dynamic-update-slice_fusion.4
  80.0 0.7 dynamic_slice.37
  82.2 1.0 constant_dynamic-slice_fusion.4
  83.3 0.6 fusion.41
  84.1 0.7 constant_dynamic-update-slice_fusion.4
  84.8 0.7 dynamic_slice.37
  87.0 1.0 constant_dynamic-slice_fusion.4
  88.2 0.6 fusion.41
  89.0 0.7 constant_dynamic-update-slice_fusion.4
  89.7 0.7 dynamic_slice.37
  91.9 1.0 constant_dynamic-slice_fusion.4
  93.0 0.6 fusion.41
  93.8 0.7 constant_dynamic-update-slice_fusion.4
  94.5 71.6 %all-to-all-done = bf16[32,512,128]{1,2,0:T(8,128)(2,1)} async-done(((bf16[32,512,128]{1,2,0:T(8,128)(2,1)}), bf16[32,512,128]{1,2,0:T(8,128)(2,1)}, u32[]{:S(2)}, u32[]{:S(2)}) %all-to-all-start) | async-done | bytes 4194336 | tf_op jit(solution)/shard_map/all_to_all | solution.py:79
  166.1 8.8 %all-gather.3.cloned.1.call-done = bf16[768,4096]{1,0:T(8,128)(2,1)} async-done(((bf16[768,512]{1,0:T(8,128)(2,1)}), bf16[768,4096]{1,0:T(8,128)(2,1)}) %all-gather.3.cloned.1.call-update) | async-done | bytes 6291472 | tf_op jit(solution)/shard_map/all_gather | solution.py:75
  175.0 8.9 %fusion.25 = (bf16[768,512]{1,0:T(8,128)(2,1)}, bf16[768,512]{1,0:T(8,128)(2,1)S(1)}) fusion(f32[6,128,512]{2,1,0:T(8,128)} %get-tuple-element.114, bf16[768,512]{1,0:T(8,128)(2,1)} %param.17, bf16[768,4096]{1,0:T(8,128)(2,1)} %all-gather.3.cloned.1.call-done, bf16[512,4096]{0,1:T(8,128)(2,1)} %bitcast.10), kind=kOutput, calls=%fused_computation.43 | convolution fusion | flops 3223191552 | bytes 14417920 | tf_op jit(solution)/shard_map/dot_general | solution.py:76
  183.9 1.5 collective-permute-start.2
  185.4 4.2 collective-permute-done.2
  189.9 24.8 %while.23 = (s32[]{:T(128)}, f32[6,128,512]{2,1,0:T(8,128)S(1)}, s32[6]{0:T(128)S(1)}, bf16[896,512]{1,0:T(8,128)(2,1)S(1)}, s32[896]{0:T(1024)S(1)}, /*index=5*...) while((s32[]{:T(128)}, f32[6,128,512]{2,1,0:T(8,128)S(1)}, s32[6]{0:T(128)S(1)}, ...), condition=%wide.region_6.7_spmd, body=%wide.region_5.6_spmd.sunk | while | flops 34635908 | bytes 4788399 | solution.py:101
  189.9 0.7 dynamic_slice.40
  191.5 2.2 fusion.44
  194.0 0.7 dynamic_slice.40
  195.6 2.4 fusion.44
  198.2 0.7 dynamic_slice.40
  199.8 2.2 fusion.44
  202.3 0.7 dynamic_slice.40
  203.9 2.3 fusion.44
  206.4 0.7 dynamic_slice.40
  208.0 2.3 fusion.44
  210.6 0.7 dynamic_slice.40
  212.2 2.2 fusion.44
  214.6 1.8 fusion.18
  216.4 164.4 %all-gather.5.cloned.1.call-done = bf16[4096,3,512]{2,0,1:T(8,128)(2,1)} async-done(((bf16[128,3,512]{2,0,1:T(8,128)(2,1)}), bf16[4096,3,512]{2,0,1:T(8,128)(2,1)}) %all-gather.5.cloned.1.call-update) | async-done | bytes 12582928 | tf_op jit(solution)/shard_map/all_gather | solution.py:107
  380.8 14.8 %bitcast_convert_fusion = bf16[768,4096]{1,0:T(8,128)(2,1)} fusion(bf16[4096,3,512]{2,0,1:T(8,128)(2,1)} %all-gather.5.cloned.1.call-done, bf16[768,1,512]{2,0,1:T(8,128)(2,1)S(1)} %bitcast.68, bf16[768,1,512]{2,0,1:T(8,128)(2,1)S(1)} %bitcast.67, bf16[768,1,512]{2,0,1:T(8,128)(2,1)} %bitcast.72), kind=kOutput, calls=%fused_computation.20 | convolution fusion | flops 9669181440 | bytes 21233664 | tf_op jit(solution)/shard_map/dot_general | solution.py:109
  395.6 0.7 copy-done.6
  396.3 67.7 %reduce-scatter.2.cloned.1.call-done = bf16[768,512]{1,0:T(8,128)(2,1)} async-done(((bf16[768,4096]{1,0:T(8,128)(2,1)}), bf16[768,512]{1,0:T(8,128)(2,1)}) %reduce-scatter.2.cloned.1.call-update) | async-done | bytes 786448 | tf_op jit(solution)/shard_map/reduce_scatter | solution.py:112
  464.0 1.6 fusion.19
  465.6 16.0 %all-reduce = (f32[768]{0:T(1024)S(1)}, f32[768]{0:T(1024)S(1)}) all-reduce(f32[768]{0:T(1024)S(1)} %get-tuple-element.153, f32[768]{0:T(1024)S(1)} %get-tuple-element.152), channel_id=1, replica_groups=mesh['ctx'=32,'ch'=8] {'ch'}, use_global_device_ids=true, to_apply=%region_9.10 | all-reduce | flops 1536 | bytes 12288 | tf_op jit(solution)/shard_map/psum | solution.py:116
  481.7 1.5 fusion.23
  (114 shorter events, 7.3 us)
Async XLA Ops:
  6.5 27.8 %copy-start = (bf16[32,128]{1,0:T(8,128)(2,1)S(1)}, bf16[32,128]{1,0:T(8,128)(2,1)}, u32[]{:S(2)}) copy-start(bf16[32,128]{1,0:T(8,128)(2,1)} %param.20) | copy-start | bytes 24580
  6.5 168.4 %all-gather.3.cloned.1.call-start = ((), (), s32[]{:S(2)}) async-start(), calls=%async_computation.2 | async-start | bytes 7077888 | tf_op jit(solution)/shard_map/all_gather | solution.py:75
  7.3 373.5 %all-gather.5.cloned.1.call-start = ((), (), s32[]{:S(2)}) async-start(), calls=%async_computation.3 | async-start | bytes 12976128 | tf_op jit(solution)/shard_map/all_gather | solution.py:107
  11.5 14.8 %copy-start.1 = (bf16[768,512]{1,0:T(8,128)(2,1)S(1)}, bf16[768,512]{1,0:T(8,128)(2,1)}, u32[]{:S(2)}) copy-start(bf16[768,512]{1,0:T(8,128)(2,1)} %param.19) | copy-start | bytes 2359300
  11.5 14.8 %copy-start.2 = (bf16[768,512]{1,0:T(8,128)(2,1)S(1)}, bf16[768,512]{1,0:T(8,128)(2,1)}, u32[]{:S(2)}) copy-start(bf16[768,512]{1,0:T(8,128)(2,1)} %param.18) | copy-start | bytes 2359300
  11.5 154.6 %all-to-all-start = ((bf16[32,512,128]{1,2,0:T(8,128)(2,1)}), bf16[32,512,128]{1,2,0:T(8,128)(2,1)}, u32[]{:S(2)}, u32[]{:S(2)}) async-start(bf16[32,512,128]{1,2,0:T(8,128)(2,1)} %stack.10), calls=%async_computation | async-start | bytes 8388608 | tf_op jit(solution)/shard_map/all_to_all | solution.py:79
  26.3 3.4 copy-start.7
  26.3 437.7 %reduce-scatter.2.cloned.1.call-start = ((), (), s32[]{:S(2)}) async-start(), calls=%async_computation.4 | async-start | bytes 7077888 | tf_op jit(solution)/shard_map/reduce_scatter | solution.py:112
  26.6 36.4 %collective-permute-start = (bf16[128,512]{1,0:T(8,128)(2,1)S(1)}, bf16[128,512]{1,0:T(8,128)(2,1)S(1)}, u32[]{:S(2)}, u32[]{:S(2)}) collective-permute-start(bf16[128,512]{1,0:T(8,128)(2,1)S(1)} %slice.20), channel_id=1, source_target_pairs={{0,8},{8,16},{16,24},{24,32},{32,40},{40,48},{48,56},{56,64},{64,7... | collective-permute-start | bytes 393224 | tf_op jit(solution)/shard_map/ppermute | solution.py:16
  30.3 30.7 %collective-permute-start.1 = (s32[1]{0:T(128)}, s32[1]{0:T(128)}, u32[]{:S(2)}, u32[]{:S(2)}) collective-permute-start(s32[1]{0:T(128)} %bitcast.12), channel_id=1, source_target_pairs={{0,8},{8,16},{16,24},{24,32},{32,40},{40,48},{48,56},{56,64},{64,7... | collective-permute-start | bytes 20 | tf_op jit(solution)/shard_map/ppermute | solution.py:16
  61.7 123.7 %collective-permute-start.3 = (s32[128]{0:T(128)S(1)}, s32[128]{0:T(128)S(1)}, u32[]{:S(2)}, u32[]{:S(2)}) collective-permute-start(s32[128]{0:T(128)S(1)} %slice.19), channel_id=1, source_target_pairs={{8,0},{16,8},{24,16},{32,24},{40,32},{48,40},{56,48},{64,56},{72,6... | collective-permute-start | bytes 1544 | tf_op jit(solution)/shard_map/ppermute | solution.py:16
  183.9 5.7 %collective-permute-start.2 = (bf16[128,512]{1,0:T(8,128)(2,1)S(1)}, bf16[128,512]{1,0:T(8,128)(2,1)S(1)}, u32[]{:S(2)}, u32[]{:S(2)}) collective-permute-start(bf16[128,512]{1,0:T(8,128)(2,1)S(1)} %slice.21), channel_id=1, source_target_pairs={{8,0},{16,8},{24,16},{32,24},{40,32},{48,40},{56,48},{64,56},{72,6... | collective-permute-start | bytes 393224 | tf_op jit(solution)/shard_map/ppermute | solution.py:16
  395.6 0.7 copy-start.6
  395.6 68.4 %copy-start.3 = (bf16[768,512]{1,0:T(8,128)(2,1)S(1)}, bf16[768,512]{1,0:T(8,128)(2,1)}, u32[]{:S(2)}) copy-start(bf16[768,512]{1,0:T(8,128)(2,1)} %param.15) | copy-start | bytes 2359300
  396.2 85.4 %copy-start.4 = (bf16[768,512]{1,0:T(8,128)(2,1)S(1)}, bf16[768,512]{1,0:T(8,128)(2,1)}, u32[]{:S(2)}) copy-start(bf16[768,512]{1,0:T(8,128)(2,1)} %param.14) | copy-start | bytes 2359300
  464.0 17.7 %copy-start.5 = (bf16[768,512]{1,0:T(8,128)(2,1)S(1)}, bf16[768,512]{1,0:T(8,128)(2,1)}, u32[]{:S(2)}) copy-start(bf16[768,512]{1,0:T(8,128)(2,1)} %reduce-scatter.2.cloned.1.call-done) | copy-start | bytes 2359300
Sparse Core Ops, SparseCore 0:
  9.1 165.7 all-gather.2
  178.5 202.2 all-gather.4
  395.7 68.2 reduce-scatter.1
